TPU v7x, 256 devices: a whole 4x4x8 slice. The times are simulated.
256 devices in a mesh: group: 8 (over y, core), dev: 32 (over z, x).
Axes of the slice: x: 4, y: 4, z: 8, core: 2. Of those that a mesh axis runs over, the one named last changes fastest.
Arguments:
- points: float32 [440, 131072], P(None, ('group', 'dev')), may hold values from -6 to 6
- residual: float32 [147, 131072], P(None, ('group', 'dev')), may hold values from -6 to 6
- coeffs: float32 [147, 131072], P(None, ('group', 'dev')), may hold values from -3 to 3
- owners: int32 [2], replicated, may hold values from 0 to 255
- offsets: int32 [2], replicated, may hold values from 0 to 256
Outputs:
- new_residual: float32 [147, 131072], P(None, ('group', 'dev'))
- new_coeffs: float32 [147, 131072], P(None, ('group', 'dev'))
All inputs are finite; a program needn't handle non-finite values.
Results may differ from a plain program's by a relative error of at most 0.0003.
Values sent between devices are 32-bit elements; how exact they have to be, the bound alone decides.
No kernel may reach another device: no remote copies, remote signals or barrier semaphores. Data moves between devices by JAX's collectives and lax.ppermute only.
A program may use at most 64 MiB of HBM per device.

v0:
```python
import jax
import jax.numpy as jnp
from jax import lax
from jax.sharding import PartitionSpec as P

BLOCK = 256
ridge = 2.0
step_norm = 1.5


def spread_2(value, axis, root):
    mine = lax.axis_index(axis) == root
    return lax.psum(jnp.where(mine, value, jnp.zeros_like(value)), axis)


def kernel_tile(cols, block):
    cross = lax.dot_general(
        block,
        cols,
        (((0,), (0,)), ((), ())),
        precision=lax.Precision.HIGHEST,
        preferred_element_type=jnp.float32,
    )
    dist = (
        jnp.sum(block * block, axis=0)[:, None]
        + jnp.sum(cols * cols, axis=0)[None, :]
        - 2.0 * cross
    )
    return jnp.exp(-dist / cols.shape[0])


def precondition(grad, block):
    gram = kernel_tile(block, block) + ridge * jnp.eye(block.shape[1], dtype=jnp.float32)
    lower = jnp.linalg.cholesky(gram)
    inner = lax.linalg.triangular_solve(lower, grad.T, left_side=True, lower=True)
    solved = lax.linalg.triangular_solve(lower, inner, left_side=True, lower=True, transpose_a=True)
    scale = step_norm / jnp.sqrt(jnp.mean(grad * grad) + 1e-06)
    return scale * solved.T


def contract(left, right):
    return lax.dot_general(
        left,
        right,
        (((1,), (1,)), ((), ())),
        precision=lax.Precision.HIGHEST,
        preferred_element_type=jnp.float32,
    )


def spread(delta, tile):
    return jnp.dot(delta, tile, precision=lax.Precision.HIGHEST, preferred_element_type=jnp.float32)


def body(points, residual, coeffs, owners, offsets):
    here = lax.axis_index(("group", "dev"))
    for step in range(2):
        local = lax.dynamic_slice_in_dim(points, offsets[step], BLOCK, 1)
        block = spread_2(local, ("group", "dev"), owners[step])
        tile = kernel_tile(points, block)
        grad = lax.psum(contract(residual, tile), ("group", "dev"))
        delta = precondition(grad, block)
        residual = residual - spread(delta, tile)
        current = lax.dynamic_slice_in_dim(coeffs, offsets[step], BLOCK, 1)
        mine = jnp.where(here == owners[step], delta, jnp.zeros_like(delta))
        coeffs = lax.dynamic_update_slice_in_dim(coeffs, current + mine, offsets[step], 1)
    return (residual, coeffs)


def solution(mesh):
    return jax.shard_map(
        body,
        mesh=mesh,
        in_specs=(
            P(None, ("group", "dev")),
            P(None, ("group", "dev")),
            P(None, ("group", "dev")),
            P(),
            P(),
        ),
        out_specs=(P(None, ("group", "dev")), P(None, ("group", "dev"))),
        check_vma=False,
    )
```

profile of v0, /device:TPU:1, one launch (start us, length us, event | category | flops | bytes accessed | tf_op | source)
XLA Modules:
  0.0 847.5 jit_solution(16834892905847499718)
XLA Ops:
  7.2 1.0 copy.40
  8.2 0.7 copy-done.7
  8.8 0.6 fusion.47
  12.0 0.6 copy-done.8
  12.7 0.7 fusion.46
  15.9 2.6 dynamic-slice_select_fusion
  18.7 256.7 %all-reduce.6.cloned.1.call-done = f32[440,256]{1,0:T(8,128)} async-done(((f32[440,256]{1,0:T(8,128)}), f32[440,256]{1,0:T(8,128)}) %all-reduce.6.cloned.1.call-update) | async-done | bytes 450576 | tf_op jit(solution)/shard_map/psum | solution.py:13
  275.4 1.2 multiply_reduce_fusion.2
  276.6 1.0 fusion.12
  277.8 11.7 %cholesky.130 = f32[128,128]{1,0:T(8,128)S(1)} custom-call(f32[128,128]{1,0:T(8,128)S(1)} %cholesky.194), custom_call_target="Cholesky" | custom-call | tf_op jit(solution)/shard_map/jit(cholesky)/cholesky | solution.py:34
  289.6 9.8 %custom-call.17 = f32[1,128,128]{1,2,0:T(8,128)S(1)} custom-call(f32[1,128,128]{2,1,0:T(8,128)S(1)} %get-tuple-element.68), custom_call_target="InvertDiagBlocksLowerTriangular" | custom-call | tf_op jit(solution)/shard_map/jit(cholesky)/cholesky | solution.py:34
  299.9 11.7 %cholesky.147 = f32[128,128]{1,0:T(8,128)S(1)} custom-call(f32[128,128]{1,0:T(8,128)S(1)} %convolution_subtract_fusion.7), custom_call_target="Cholesky" | custom-call | tf_op jit(solution)/shard_map/jit(cholesky)/cholesky | solution.py:34
  311.6 12.0 %fusion.7 = f32[256,512]{1,0:T(8,128)S(1)} fusion(f32[440,256]{1,0:T(8,128)S(1)} %copy-done.2, f32[440,512]{1,0:T(8,128)S(1)} %copy-done, f32[512]{0:T(512)S(1)} %multiply_reduce_fusion, f32[256]{0:T(256)S(1)} %multiply_reduce_fusion.2), kind=kOutput, calls=%fused_computation.13 | convolution fusion | flops 692715520 | bytes 1879040 | tf_op jit(solution)/shard_map/dot_general | solution.py:17
  323.7 1.3 convolution_bitcast_fusion
  325.1 0.7 compare_reduce_fusion.2
  327.2 4.0 while.8
  327.2 0.6 fusion.79
  327.8 1.4 bitcast_dynamic-update-slice_fusion.4
  329.2 0.6 fusion.79
  329.8 1.4 bitcast_dynamic-update-slice_fusion.4
  331.2 19.7 %custom-call.19 = f32[2,128,128]{1,2,0:T(8,128)S(1)} custom-call(f32[2,128,128]{2,1,0:T(8,128)S(1)} %get-tuple-element.34), custom_call_target="InvertDiagBlocksLowerTriangular" | custom-call | tf_op jit(solution)/shard_map/triangular_solve/custom-call.4 | solution.py:36
  350.9 226.4 %all-reduce.10.cloned.1.call-done = (f32[147,256]{1,0:T(8,128)}, f32[440,256]{1,0:T(8,128)}) async-done(((f32[147,256]{1,0:T(8,128)}, f32[440,256]{1,0:T(8,128)}), (f32[147,256]{1,0:T(8,128)}, f32[440,256]{1,0:T(8,128)})) %all-reduce.10.cloned.1.call-update) | async-done | bytes 601104 | tf_op jit(solution)/shard_map/psum | solution.py:61
  577.3 1.2 multiply_reduce_fusion.1
  578.5 1.2 fusion.5
  579.7 1.0 fusion.17
  580.7 0.6 multiply_reduce_fusion.4
  581.6 0.3 convolution_subtract_fusion.5
  582.8 0.3 fusion.32
  583.8 0.5 convolution_subtract_fusion.1
  584.3 1.4 fusion.48
  585.8 11.7 %cholesky.164 = f32[128,128]{1,0:T(8,128)S(1)} custom-call(f32[128,128]{1,0:T(8,128)S(1)} %cholesky.197), custom_call_target="Cholesky" | custom-call | tf_op jit(solution)/shard_map/jit(cholesky)/cholesky | solution.py:34
  597.6 9.8 %custom-call.20 = f32[1,128,128]{1,2,0:T(8,128)S(1)} custom-call(f32[1,128,128]{2,1,0:T(8,128)S(1)} %get-tuple-element.64), custom_call_target="InvertDiagBlocksLowerTriangular" | custom-call | tf_op jit(solution)/shard_map/jit(cholesky)/cholesky | solution.py:34
  607.9 11.9 %cholesky.181 = f32[128,128]{1,0:T(8,128)S(1)} custom-call(f32[128,128]{1,0:T(8,128)S(1)} %convolution_subtract_fusion.6), custom_call_target="Cholesky" | custom-call | tf_op jit(solution)/shard_map/jit(cholesky)/cholesky | solution.py:34
  619.8 0.7 compare_reduce_fusion
  621.9 4.0 while.9
  621.9 0.6 fusion.80
  622.5 1.4 bitcast_dynamic-update-slice_fusion.5
  623.9 0.6 fusion.80
  624.4 1.4 bitcast_dynamic-update-slice_fusion.5
  625.8 19.7 %custom-call.22 = f32[2,128,128]{1,2,0:T(8,128)S(1)} custom-call(f32[2,128,128]{2,1,0:T(8,128)S(1)} %get-tuple-element.36), custom_call_target="InvertDiagBlocksLowerTriangular" | custom-call | tf_op jit(solution)/shard_map/triangular_solve/custom-call.4 | solution.py:36
  645.6 1.5 dynamic_update_slice.6
  647.1 185.8 %all-reduce.8.cloned.1.call-done = f32[147,256]{1,0:T(8,128)} async-done(((f32[147,256]{1,0:T(8,128)}), f32[147,256]{1,0:T(8,128)}) %all-reduce.8.cloned.1.call-update) | async-done | bytes 150544 | tf_op jit(solution)/shard_map/psum | solution.py:61
  832.9 1.2 fusion.20
  834.8 0.3 fusion.37
  835.7 0.6 multiply_reduce_fusion.3
  837.0 1.2 convolution_subtract_fusion
  838.3 1.5 dynamic_update_slice.7
  839.8 0.7 copy-done.4
  (58 shorter events, 4.5 us)
Async XLA Ops:
  7.2 268.3 %all-reduce.6.cloned.1.call-start = ((), (), s32[]{:S(2)}) async-start(), calls=%async_computation | async-start | bytes 901120 | tf_op jit(solution)/shard_map/psum | solution.py:13
  8.2 0.7 copy-start.7
  12.0 0.7 copy-start.8
  15.9 2.7 copy-start
  18.5 558.8 %all-reduce.10.cloned.1.call-start = ((), (), s32[]{:S(2)}) async-start(), calls=%async_computation.2 | async-start | bytes 1212416 | tf_op jit(solution)/shard_map/psum | solution.py:61
  275.4 1.2 copy-start.2
  311.6 12.0 %copy-start.3 = (f32[147,512]{1,0:T(8,128)S(1)}, f32[147,512]{1,0:T(8,128)}, u32[]{:S(2)}) copy-start(f32[147,512]{1,0:T(8,128)} %param.11) | copy-start | bytes 903172
  325.0 507.9 %all-reduce.8.cloned.1.call-start = ((), (), s32[]{:S(2)}) async-start(), calls=%async_computation.1 | async-start | bytes 311296 | tf_op jit(solution)/shard_map/psum | solution.py:61
  577.3 1.2 copy-start.1
  579.6 1.0 copy-start.6
  832.9 1.2 copy-start.5
  839.8 0.7 copy-start.4
Sparse Core Ops, SparseCore 0:
  18.7 256.7 all-reduce.5
  325.1 252.1 all-reduce.9
  585.8 247.1 all-reduce.7
where the time goes:
time: 857 us; the launch traced here: 847 us
  waiting for transfers between devices  669 us (78%)
  other arithmetic  114 us (13%)
  matrix products  24.9 us (3%)
  between operations  23.6 us (3%)
  local copies, waits for them, and re-layouts  15.5 us (2%)
    psum x2, waiting for transfers between devices, body(): grad = lax.psum(contract(residual, tile), ('group', 'dev'))  412 us
    psum x1, waiting for transfers between devices, spread_2(): return lax.psum(jnp.where(mine, value, jnp.zeros_like(value)), axis)  257 us
    another operation x12, other arithmetic, precondition(): lower = jnp.linalg.cholesky(gram)  68.2 us
    another operation x5, other arithmetic, precondition(): lax.linalg.triangular_solve(lower, inner, left_side=True, lower=True, tra...  39.4 us
  transfers between devices with their start and end apart: 3, of which 3 were waited for; matrix products, arithmetic and copies ran while one was open for 10% of the time, Pallas kernels for 0%

commit v1 on v0

--- a/solution.py
+++ b/solution.py
@@ -1,3 +1,4 @@
+import functools
 import jax
 import jax.numpy as jnp
 from jax import lax
@@ -6,6 +7,15 @@
 BLOCK = 256
 ridge = 2.0
 step_norm = 1.5
+
+
+def hold_map(inputs, which_axis, comm_axis):
+    for k0 in (which_axis, comm_axis):
+        inputs = lax.psum(inputs, axis_name=k0)
+    return inputs
+
+
+name_target_on_mesh = functools.partial(hold_map, which_axis="dev", comm_axis="group")
 
 
 def spread_2(value, axis, root):
@@ -58,7 +68,7 @@
         local = lax.dynamic_slice_in_dim(points, offsets[step], BLOCK, 1)
         block = spread_2(local, ("group", "dev"), owners[step])
         tile = kernel_tile(points, block)
-        grad = lax.psum(contract(residual, tile), ("group", "dev"))
+        grad = name_target_on_mesh(contract(residual, tile))
         delta = precondition(grad, block)
         residual = residual - spread(delta, tile)
         current = lax.dynamic_slice_in_dim(coeffs, offsets[step], BLOCK, 1)

time: 857 us -> 720 us (0.84)
  waiting for transfers between devices: 669 us -> 544 us
  matrix products: 24.9 us -> 15.3 us
    psum x2 -> x4, waiting for transfers between devices: 412 us -> 285 us  [hold_map(): inputs = lax.psum(inputs, axis_name=k0)]
    dot_general x4, matrix products: 15.2 us -> 4.62 us  [kernel_tile(): lax.dot_general(block, cols, (((0,), (0,)), ((), ())), precision=lax.Prec...]
  transfers between devices with their start and end apart: 3 -> 5, of which waited for: 3 -> 5; matrix products, arithmetic and copies ran while one was open for 10% -> 17% of each run, Pallas kernels for 0% -> 0%
where the time goes in v1:
time: 720 us; the launch traced here: 716 us
  waiting for transfers between devices  544 us (76%)
  other arithmetic  114 us (16%)
  between operations  23.5 us (3%)
  local copies, waits for them, and re-layouts  18.6 us (3%)
  matrix products  15.3 us (2%)
    psum x4, waiting for transfers between devices, hold_map(): inputs = lax.psum(inputs, axis_name=k0)  285 us
    psum x1, waiting for transfers between devices, spread_2(): return lax.psum(jnp.where(mine, value, jnp.zeros_like(value)), axis)  259 us
    another operation x12, other arithmetic, precondition(): lower = jnp.linalg.cholesky(gram)  68 us
    another operation x5, other arithmetic, precondition(): lax.linalg.triangular_solve(lower, inner, left_side=True, lower=True, tra...  40.2 us
  transfers between devices with their start and end apart: 5, of which 5 were waited for; matrix products, arithmetic and copies ran while one was open for 17% of the time, Pallas kernels for 0%

profile of v1, /device:TPU:1, one launch (start us, length us, event | category | flops | bytes accessed | tf_op | source)
XLA Modules:
  0.0 716.2 jit_solution(139602668222635119)
XLA Ops:
  7.2 1.0 copy.42
  8.2 0.7 copy-done.10
  12.0 0.6 copy-done.11
  12.7 0.7 fusion.46
  15.9 2.6 dynamic-slice_select_fusion
  18.5 1.1 copy-done
  19.7 259.5 %all-reduce.16.cloned.1.call-done = (f32[440,256]{1,0:T(8,128)}, f32[440,256]{1,0:T(8,128)}) async-done(((f32[440,256]{1,0:T(8,128)}, f32[440,256]{1,0:T(8,128)}), (f32[440,256]{1,0:T(8,128)}, f32[440,256]{1,0:T(8,128)})) %all-reduce.16.cloned.1.call-update) | async-done | bytes 901136 | tf_op jit(solution)/shard_map/psum | solution.py:23
  279.2 1.2 multiply_reduce_fusion.2
  280.4 1.0 fusion.12
  281.4 1.2 fusion.7
  282.6 1.3 convolution_bitcast_fusion
  284.7 11.7 %cholesky.130 = f32[128,128]{1,0:T(8,128)S(1)} custom-call(f32[128,128]{1,0:T(8,128)S(1)} %cholesky.194), custom_call_target="Cholesky" | custom-call | tf_op jit(solution)/shard_map/jit(cholesky)/cholesky | solution.py:44
  296.5 9.8 %custom-call.17 = f32[1,128,128]{1,2,0:T(8,128)S(1)} custom-call(f32[1,128,128]{2,1,0:T(8,128)S(1)} %get-tuple-element.68), custom_call_target="InvertDiagBlocksLowerTriangular" | custom-call | tf_op jit(solution)/shard_map/jit(cholesky)/cholesky | solution.py:44
  306.8 11.7 %cholesky.147 = f32[128,128]{1,0:T(8,128)S(1)} custom-call(f32[128,128]{1,0:T(8,128)S(1)} %convolution_subtract_fusion.7), custom_call_target="Cholesky" | custom-call | tf_op jit(solution)/shard_map/jit(cholesky)/cholesky | solution.py:44
  318.5 0.7 compare_reduce_fusion.2
  320.6 4.2 while.8
  320.6 0.6 fusion.79
  321.3 1.3 bitcast_dynamic-update-slice_fusion.4
  322.6 0.6 fusion.79
  323.3 1.3 bitcast_dynamic-update-slice_fusion.4
  324.8 0.6 copy-done.9
  325.5 1.0 fusion.17
  326.8 0.7 copy-done.5
  327.5 11.7 %cholesky.164 = f32[128,128]{1,0:T(8,128)S(1)} custom-call(f32[128,128]{1,0:T(8,128)S(1)} %cholesky.197), custom_call_target="Cholesky" | custom-call | tf_op jit(solution)/shard_map/jit(cholesky)/cholesky | solution.py:44
  339.2 9.8 %custom-call.20 = f32[1,128,128]{1,2,0:T(8,128)S(1)} custom-call(f32[1,128,128]{2,1,0:T(8,128)S(1)} %get-tuple-element.64), custom_call_target="InvertDiagBlocksLowerTriangular" | custom-call | tf_op jit(solution)/shard_map/jit(cholesky)/cholesky | solution.py:44
  349.5 11.7 %cholesky.181 = f32[128,128]{1,0:T(8,128)S(1)} custom-call(f32[128,128]{1,0:T(8,128)S(1)} %convolution_subtract_fusion.6), custom_call_target="Cholesky" | custom-call | tf_op jit(solution)/shard_map/jit(cholesky)/cholesky | solution.py:44
  361.3 0.7 compare_reduce_fusion
  363.4 1.4 fusion.5
  364.8 57.1 %all-reduce.8.cloned.1.call-done = f32[147,256]{1,0:T(8,128)} async-done(((f32[147,256]{1,0:T(8,128)}), f32[147,256]{1,0:T(8,128)}) %all-reduce.8.cloned.1.call-update) | async-done | bytes 150544 | tf_op jit(solution)/shard_map/psum | solution.py:14
  422.0 20.5 %custom-call.19 = f32[2,128,128]{1,2,0:T(8,128)S(1)} custom-call(f32[2,128,128]{2,1,0:T(8,128)} %copy-done.9), custom_call_target="InvertDiagBlocksLowerTriangular" | custom-call | tf_op jit(solution)/shard_map/triangular_solve/custom-call.4 | solution.py:46
  442.5 47.3 %all-reduce.10.cloned.1.call-done = f32[147,256]{1,0:T(8,128)} async-done(((f32[147,256]{1,0:T(8,128)}), f32[147,256]{1,0:T(8,128)}) %all-reduce.10.cloned.1.call-update) | async-done | bytes 150544 | tf_op jit(solution)/shard_map/psum | solution.py:14
  489.8 1.2 fusion.22
  492.5 0.6 multiply_reduce_fusion.4
  494.3 1.4 fusion.48
  495.8 0.6 copy-done.13
  496.4 3.9 while.9
  496.4 0.6 fusion.80
  497.0 1.4 bitcast_dynamic-update-slice_fusion.5
  498.9 1.4 bitcast_dynamic-update-slice_fusion.5
  500.3 19.7 %custom-call.22 = f32[2,128,128]{1,2,0:T(8,128)S(1)} custom-call(f32[2,128,128]{2,1,0:T(8,128)S(1)} %get-tuple-element.36), custom_call_target="InvertDiagBlocksLowerTriangular" | custom-call | tf_op jit(solution)/shard_map/triangular_solve/custom-call.4 | solution.py:46
  520.0 114.1 %all-reduce.12.cloned.1.call-done = f32[147,256]{1,0:T(8,128)} async-done(((f32[147,256]{1,0:T(8,128)}), f32[147,256]{1,0:T(8,128)}) %all-reduce.12.cloned.1.call-update) | async-done | bytes 150544 | tf_op jit(solution)/shard_map/psum | solution.py:14
  634.2 1.5 dynamic_update_slice.6
  635.7 66.1 %all-reduce.14.cloned.1.call-done = f32[147,256]{1,0:T(8,128)} async-done(((f32[147,256]{1,0:T(8,128)}), f32[147,256]{1,0:T(8,128)}) %all-reduce.14.cloned.1.call-update) | async-done | bytes 150544 | tf_op jit(solution)/shard_map/psum | solution.py:14
  701.8 1.2 fusion.20
  704.5 0.6 multiply_reduce_fusion.3
  705.9 1.2 convolution_subtract_fusion
  707.2 1.5 dynamic_update_slice.7
  708.7 0.7 copy-done.4
  (74 shorter events, 7.4 us)
Async XLA Ops:
  7.2 272.0 %all-reduce.16.cloned.1.call-start = ((), (), s32[]{:S(2)}) async-start(), calls=%async_computation.4 | async-start | bytes 1802240 | tf_op jit(solution)/shard_map/psum | solution.py:23
  8.2 0.7 copy-start.10
  12.0 0.7 copy-start.11
  18.5 1.2 copy-start
  18.5 403.4 %all-reduce.8.cloned.1.call-start = ((), (), s32[]{:S(2)}) async-start(), calls=%async_computation | async-start | bytes 311296 | tf_op jit(solution)/shard_map/psum | solution.py:14
  279.2 1.2 copy-start.2
  281.4 1.2 copy-start.3
  284.0 205.8 %all-reduce.10.cloned.1.call-start = ((), (), s32[]{:S(2)}) async-start(), calls=%async_computation.1 | async-start | bytes 311296 | tf_op jit(solution)/shard_map/psum | solution.py:14
  320.5 5.0 copy-start.1
  324.8 0.6 copy-start.9
  324.8 0.7 copy-start.12
  326.7 0.7 copy-start.5
  327.5 21.6 %copy-start.6 = (f32[256,256]{1,0:T(8,128)S(1)}, f32[256,256]{1,0:T(8,128)}, u32[]{:S(2)}) copy-start(f32[256,256]{1,0:T(8,128)} %copy-done.5) | copy-start | bytes 786436
  421.9 212.1 %all-reduce.12.cloned.1.call-start = ((), (), s32[]{:S(2)}) async-start(), calls=%async_computation.2 | async-start | bytes 311296 | tf_op jit(solution)/shard_map/psum | solution.py:14
  489.8 1.2 copy-start.7
  495.7 0.7 copy-start.13
  495.7 206.1 %all-reduce.14.cloned.1.call-start = ((), (), s32[]{:S(2)}) async-start(), calls=%async_computation.3 | async-start | bytes 311296 | tf_op jit(solution)/shard_map/psum | solution.py:14
  701.8 1.2 copy-start.8
  708.7 0.7 copy-start.4
Sparse Core Ops, SparseCore 0:
  18.6 260.5 all-reduce.15
  284.1 137.7 all-reduce.7
  424.3 65.4 all-reduce.9
  495.8 138.1 all-reduce.11
  636.3 65.5 all-reduce.13
